TPU v7x, 256 devices: a whole 4x4x8 slice. The times are simulated.
256 devices in a mesh: head: 8 (over z), outer: 2 (over core), inner: 16 (over y, x).
Axes of the slice: x: 4, y: 4, z: 8, core: 2. Of those that a mesh axis runs over, the one named last changes fastest.
Arguments:
- query: bfloat16 [8192, 64, 128], P(('outer', 'inner'), 'head'), may hold values from -24 to 24
- keys: bfloat16 [8192, 8, 128], P(('outer', 'inner'), 'head'), may hold values from -8 to 8
- values: bfloat16 [8192, 8, 128], P(('outer', 'inner'), 'head'), may hold values from -6 to 6
- forward_output: bfloat16 [8192, 64, 128], P(('outer', 'inner'), 'head'), may hold values from -2.390625 to 2.390625
- d_out: bfloat16 [8192, 64, 128], P(('outer', 'inner'), 'head'), may hold values from -2.390625 to 2.390625
- span_order: int32 [1, 32], replicated, may hold values from 0 to 31, each once within a row
Outputs:
- d_query: bfloat16 [32, 256, 64, 128], P(('outer', 'inner'), 'head')
- key_gradient: bfloat16 [32, 256, 8, 128], P(('outer', 'inner'), 'head')
- value_gradient: bfloat16 [32, 256, 8, 128], P(('outer', 'inner'), 'head')
Inputs may be any that keep to these rules, and one draw needn't show every extreme that they name: `span_order`: each row holds every number once.
All inputs are finite; a program needn't handle non-finite values.
Results may differ from a plain program's by a relative error of at most 0.0051.
Values may be sent and summed in bfloat16 or wider, within the bound.
A program may use at most 64 MiB of HBM per device.

v0:
```python
import functools

import jax
import jax.numpy as jnp
from jax import lax
from jax.experimental import pallas as pl
from jax.experimental.pallas import tpu as pltpu
from jax.sharding import PartitionSpec as P

NB, RB, HD, PIECE, QC = 32, 256, 128, 64, 256
NG = NB * PIECE // QC
PER = QC // PIECE
NT = (((1,), (1,)), ((), ()))
TN = (((0,), (0,)), ((), ()))
NN = (((1,), (0,)), ((), ()))
F32, BF16 = jnp.float32, jnp.bfloat16
NEG = -1e30
SCALE = HD ** -0.5
SCALE2 = SCALE * 1.4426950408889634


def dot(a, b, dims):
    return lax.dot_general(a, b, dims, preferred_element_type=F32)


def fill_positions(inv, q_ref, do_ref, dl_ref, qpos, dopos, dlpos):
    for p in range(NB):
        c = inv[p]
        qpos[p * PIECE:(p + 1) * PIECE, :] = q_ref[c].reshape(PIECE, HD)
        dopos[p * PIECE:(p + 1) * PIECE, :] = do_ref[c].reshape(PIECE, HD)
    for p in range(0, NB, 2):
        both = jnp.concatenate([dl_ref[inv[p]][:, :PIECE], dl_ref[inv[p + 1]][:, :PIECE]], axis=1)
        g, off = divmod(p * PIECE, QC)
        dlpos[g, :, off:off + 128] = both


def make_visible(me, shape, shift):
    j = lax.broadcasted_iota(jnp.int32, shape, 1)
    u = lax.broadcasted_iota(jnp.int32, shape, 0)
    row = (j // PIECE) * RB + ((j % PIECE) // 8) * NB + me
    return u + shift <= row


def grads_kernel(variant, inv, me_ref, q_ref, do_ref, dl_ref, kv_ref, dq_ref, dkv_ref,
                 qpos, dopos, dlpos, lse, dqacc, dkacc, dvacc):
    me = me_ref[0]
    fill_positions(inv, q_ref, do_ref, dl_ref, qpos, dopos, dlpos)

    def fold(state, s):
        m, l = state
        s3 = s.reshape(s.shape[0] // 8, 8, QC)
        mn = jnp.maximum(m, jnp.max(s3, axis=0))
        l = l * jnp.exp2(m - mn) + jnp.sum(jnp.exp2(s3 - mn[None]), axis=0)
        return mn, l

    def chunk_total(g, _):
        qg = qpos[pl.ds(pl.multiple_of(g * QC, QC), QC), :]
        state = (jnp.full((8, QC), NEG, F32), jnp.zeros((8, QC), F32))

        def four(t, state):
            for e in range(PER):
                state = fold(state, dot(kv_ref[slot_of(inv[t * PER + e]), 0], qg, NT) * SCALE2)
            return state
        state = lax.fori_loop(0, g, four, state)
        for e in range(PER):
            s = dot(kv_ref[slot_of(inv[g * PER + e]), 0], qg, NT) * SCALE2
            state = fold(state, jnp.where(make_visible(me, s.shape, e * RB), s, NEG))
        m, l = state
        top = jnp.max(m, axis=0, keepdims=True)
        lse[g] = top + jnp.log2(jnp.sum(l * jnp.exp2(m - top), axis=0, keepdims=True))
        return 0
    lax.fori_loop(0, NG, chunk_total, 0)

    dqacc[...] = jnp.zeros_like(dqacc)

    def key_block(p, _):
        c = slot_of(inv[p])
        kb, vb = kv_ref[c, 0], kv_ref[c, 1]
        first = p // PER
        if variant == "T":
            kt = kb.T

        def visit(g, masked):
            rows = pl.ds(pl.multiple_of(g * QC, QC), QC)
            qg, dog = qpos[rows, :], dopos[rows, :]
            s = dot(kb, qg, NT) * SCALE2 - lse[g]
            w = jnp.exp2(s)
            if masked:
                w = jnp.where(make_visible(me, s.shape, (p - g * PER) * RB), w, 0.0)
            dv = dot(w.astype(BF16), dog, NN)
            ds = (w * (dot(vb, dog, NT) - dlpos[g])).astype(BF16)
            dk = dot(ds, qg, NN)
            if variant == "T":
                dqacc[g] += dot(kt, ds, NN)
            else:
                dqacc[g] += dot(ds, kb, TN)
            return dk, dv
        dk, dv = visit(first, True)
        dkacc[...] = dk
        dvacc[...] = dv

        def rest(g, _):
            dk, dv = visit(g, False)
            dkacc[...] += dk
            dvacc[...] += dv
            return 0
        lax.fori_loop(first + 1, NG, rest, 0)
        dkv_ref[c, 0] = (dkacc[...] * SCALE).astype(BF16)
        dkv_ref[c, 1] = dvacc[...].astype(BF16)
        return 0
    lax.fori_loop(0, NB, key_block, 0)

    for p in range(NB):
        g, e = divmod(p, PER)
        if variant == "T":
            if e == 0:
                whole = dqacc[g].T
            part = whole[e * PIECE:(e + 1) * PIECE, :]
        else:
            part = dqacc[g, e * PIECE:(e + 1) * PIECE, :]
        dq_ref[inv[p]] = (part * SCALE).astype(BF16)


def grads(variant, inv, me, q, do, dl, kv):
    acc = (NG, HD, QC) if variant == "T" else (NG, QC, HD)
    vm = pl.BlockSpec(memory_space=pltpu.VMEM)
    sm = pl.BlockSpec(memory_space=pltpu.SMEM)
    return pl.pallas_call(
        functools.partial(grads_kernel, variant),
        out_shape=(jax.ShapeDtypeStruct((NB, PIECE, HD), BF16),
                   jax.ShapeDtypeStruct((NB, 2, RB, HD), BF16)),
        in_specs=[sm, sm, vm, vm, vm, vm],
        out_specs=(vm, vm),
        scratch_shapes=[
            pltpu.VMEM((NB * PIECE, HD), BF16), pltpu.VMEM((NB * PIECE, HD), BF16), pltpu.VMEM((NG, 1, QC), F32),
            pltpu.VMEM((NG, 1, QC), F32), pltpu.VMEM(acc, F32),
            pltpu.VMEM((RB, HD), F32), pltpu.VMEM((RB, HD), F32)],
        compiler_params=pltpu.CompilerParams(vmem_limit_bytes=60 << 20),
        name="grads_" + variant,
    )(inv, me, q, do, dl, kv)


MESH = pl.DeviceIdType.MESH


def place():
    core = lax.axis_index("outer")
    inner = lax.axis_index("inner")
    y, x = inner // 4, lax.rem(inner, 4)
    return core, x + core * (y - x), y + core * (x - y)


def chip_at(core, a, b):
    return a + core * (4 * a + b - a) + (1 - core) * 4 * b


def slot_of(c):
    core, inner = c // 16, c % 16
    y, x = inner // 4, inner % 4
    return core * 16 + 4 * (x + core * (y - x)) + y + core * (x - y)


def turn(v, step):
    return lax.rem(v + step + 4, 4)


def greet(with_heads):
    me = lax.axis_index("outer") * 16 + lax.axis_index("inner")
    barrier = pltpu.get_barrier_semaphore()

    def one(n, _):
        to = lax.rem(me + n, NB)
        pl.semaphore_signal(barrier, inc=1, device_id={"outer": to // 16, "inner": lax.rem(to, 16)}, device_id_type=MESH)
        return 0
    lax.fori_loop(1, NB, one, 0)
    count = NB - 1
    if with_heads:
        z = lax.axis_index("head")

        def head(n, _):
            pl.semaphore_signal(barrier, inc=1, device_id={"head": lax.rem(z + n, 8)}, device_id_type=MESH)
            return 0
        lax.fori_loop(1, 8, head, 0)
        count += 7
    pl.semaphore_wait(barrier, count)
    return me


def wait_bytes(ref, sem):
    pltpu.make_async_copy(ref, ref, sem).wait()


def spread_kernel(k_ref, v_ref, q_ref, do_ref, dl_ref, kv_ref, qo_ref, doo_ref, dlo_ref,
                  kv_send, kv_recv, sib_send, sib_recv, row_send, row_recv, own_sem):
    core, al, be = place()
    me = greet(False)

    def slot(a, b):
        return core * 16 + turn(al, a) * 4 + turn(be, b)

    def to(a, b):
        return {"inner": chip_at(core, turn(al, a), turn(be, b))}
    mine = slot(0, 0)
    own = [pltpu.make_async_copy(k_ref, kv_ref.at[mine, 0], own_sem.at[0]),
           pltpu.make_async_copy(v_ref, kv_ref.at[mine, 1], own_sem.at[1]),
           pltpu.make_async_copy(q_ref.at[:, me], qo_ref.at[me], own_sem.at[2]),
           pltpu.make_async_copy(do_ref.at[:, me], doo_ref.at[me], own_sem.at[3]),
           pltpu.make_async_copy(dl_ref.at[me], dlo_ref.at[me], own_sem.at[4])]
    for c in own:
        c.start()
    own[0].wait()
    own[1].wait()
    started = []

    def send(ref, n, dev):
        c = pltpu.make_async_remote_copy(src_ref=ref, dst_ref=ref, send_sem=kv_send.at[n], recv_sem=kv_recv.at[n],
                                         device_id=dev, device_id_type=MESH)
        c.start()
        started.append(c)

    def arrived(ref, n):
        wait_bytes(ref, kv_recv.at[n])

    def to_sibling(a, b):
        n = turn(al, a) * 4 + turn(be, b)
        c = pltpu.make_async_remote_copy(
            src_ref=kv_ref.at[slot(a, b)], dst_ref=kv_ref.at[slot(a, b)], send_sem=sib_send.at[n], recv_sem=sib_recv.at[n],
            device_id={"outer": 1 - core}, device_id_type=MESH)
        c.start()
        started.append(c)

    def whole(a, b):
        return kv_ref.at[slot(a, b)]

    def half(a, b, h):
        return kv_ref.at[slot(a, b), h]
    send(whole(0, 0), 0, to(1, 0))
    send(whole(0, 0), 1, to(-1, 0))
    send(whole(0, 0), 4, to(0, 1))
    send(whole(0, 0), 5, to(0, -1))
    to_sibling(0, 0)

    def rows(n, _):
        other = lax.rem(me + n, NB)
        dev = {"outer": other // 16, "inner": lax.rem(other, 16)}
        for j, (src, dst) in enumerate(((q_ref.at[:, other], qo_ref), (do_ref.at[:, other], doo_ref), (dl_ref.at[other], dlo_ref))):
            pltpu.make_async_remote_copy(src_ref=src, dst_ref=dst.at[me], send_sem=row_send.at[j], recv_sem=row_recv.at[j],
                                         device_id=dev, device_id_type=MESH).start()
        return 0

    arrived(whole(-1, 0), 0)
    send(half(-1, 0, 0), 2, to(1, 0))
    send(whole(-1, 0), 8, to(0, 1))
    send(whole(-1, 0), 9, to(0, -1))
    to_sibling(-1, 0)
    arrived(whole(1, 0), 1)
    send(half(1, 0, 1), 3, to(-1, 0))
    send(whole(1, 0), 12, to(0, 1))
    send(whole(1, 0), 13, to(0, -1))
    to_sibling(1, 0)
    lax.fori_loop(1, NB, rows, 0)
    base = {0: 4, -1: 8, 1: 12, 2: 16}
    for a in (0, -1, 1, 2):
        n = base[a]
        if a == 2:
            arrived(half(2, 0, 0), 2)
            arrived(half(2, 0, 1), 3)
            send(whole(2, 0), 16, to(0, 1))
            send(whole(2, 0), 17, to(0, -1))
            to_sibling(2, 0)
        arrived(whole(a, -1), n)
        send(half(a, -1, 0), n + 2, to(0, 1))
        to_sibling(a, -1)
        arrived(whole(a, 1), n + 1)
        send(half(a, 1, 1), n + 3, to(0, -1))
        to_sibling(a, 1)
    for a in (0, -1, 1, 2):
        arrived(half(a, 2, 0), base[a] + 2)
        arrived(half(a, 2, 1), base[a] + 3)
        to_sibling(a, 2)
    for n in range(16):
        wait_bytes(kv_ref.at[(1 - core) * 16 + n], sib_recv.at[n])
    for c in started:
        c.wait_send()
    for j, ref in enumerate((qo_ref, doo_ref, dlo_ref)):
        wait_bytes(ref.at[pl.ds(0, NB - 1)], row_recv.at[j])
        wait_bytes(ref.at[pl.ds(0, NB - 1)], row_send.at[j])
    for c in own[2:]:
        c.wait()


def spread(k, v, q, do, dl):
    vm = pl.BlockSpec(memory_space=pltpu.VMEM)
    dma = pltpu.SemaphoreType.DMA
    return pl.pallas_call(
        spread_kernel,
        out_shape=(jax.ShapeDtypeStruct((NB, 2, RB, HD), BF16), jax.ShapeDtypeStruct((NB, 8, 8, HD), BF16),
                   jax.ShapeDtypeStruct((NB, 8, 8, HD), BF16), jax.ShapeDtypeStruct((NB, 1, HD), F32)),
        in_specs=[vm] * 5, out_specs=(vm,) * 4,
        scratch_shapes=[dma((20,)), dma((20,)), dma((16,)), dma((16,)), dma((3,)), dma((3,)), dma((5,))],
        compiler_params=pltpu.CompilerParams(collective_id=0, has_side_effects=True, vmem_limit_bytes=40 << 20),
        name="spread",
    )(k, v, q, do, dl)


def total(*parts):
    out = parts[0].astype(F32)
    for p in parts[1:]:
        out = out + p.astype(F32)
    return out


def collect_kernel(dq_ref, dkv_ref, oq_ref, okv_ref, sib, sums, from_a, opp_a, line, from_b, opp_b, mid, fin, dz,
                   sib_send, sib_recv, a_send, a_recv, b_send, b_recv, z_send, z_recv, x_send, x_recv, own_sem):
    core, al, be = place()
    z = lax.axis_index("head")
    me = greet(True)
    started = []

    def remote(src, dst, ssem, rsem, dev):
        c = pltpu.make_async_remote_copy(src_ref=src, dst_ref=dst, send_sem=ssem, recv_sem=rsem,
                                         device_id=dev, device_id_type=MESH)
        c.start()
        started.append(c)

    def to(a, b):
        return {"inner": chip_at(core, turn(al, a), turn(be, b))}
    order = (2, 1, -1, 0)
    s_al = be
    for n, a in enumerate(order):
        unit = turn(s_al, a)
        remote(dkv_ref.at[pl.ds((1 - core) * 16 + unit * 4, 4)], sib.at[n], sib_send.at[n], sib_recv.at[n], {"outer": 1 - core})

    def heads(n, _):
        other = lax.rem(z + n, 8)
        pltpu.make_async_remote_copy(src_ref=dq_ref.at[:, other], dst_ref=dz.at[:, z], send_sem=z_send.at[0],
                                     recv_sem=z_recv.at[0], device_id={"head": other}, device_id_type=MESH).start()
        return 0
    lax.fori_loop(1, 8, heads, 0)
    own_q = pltpu.make_async_copy(dq_ref.at[:, z], dz.at[:, z], own_sem.at[0])
    own_q.start()

    def mine(a):
        return dkv_ref[pl.ds(core * 16 + turn(al, a) * 4, 4)]
    wait_bytes(sib.at[0], sib_recv.at[0])
    sums[0] = total(mine(2), sib[0]).astype(BF16)
    remote(sums.at[0, :, 0], opp_a.at[0], a_send.at[0], a_recv.at[0], to(1, 0))
    remote(sums.at[0, :, 1], opp_a.at[1], a_send.at[1], a_recv.at[1], to(-1, 0))
    wait_bytes(sib.at[1], sib_recv.at[1])
    wait_bytes(sib.at[2], sib_recv.at[2])
    first, second = mine(1), mine(-1)
    sums[1, :, 1] = total(first[:, 1], sib[1, :, 1]).astype(BF16)
    sums[2, :, 0] = total(second[:, 0], sib[2, :, 0]).astype(BF16)
    wait_bytes(opp_a.at[0], a_recv.at[0])
    sums[1, :, 0] = total(first[:, 0], sib[1, :, 0], opp_a[0]).astype(BF16)
    remote(sums.at[1], from_a.at[0], a_send.at[2], a_recv.at[2], to(1, 0))
    wait_bytes(opp_a.at[1], a_recv.at[1])
    sums[2, :, 1] = total(second[:, 1], sib[2, :, 1], opp_a[1]).astype(BF16)
    remote(sums.at[2], from_a.at[1], a_send.at[3], a_recv.at[3], to(-1, 0))
    wait_bytes(sib.at[3], sib_recv.at[3])
    line[...] = total(mine(0), sib[3])
    wait_bytes(dz.at[:, pl.ds(0, 7)], z_recv.at[0])
    own_q.wait()

    def rows(n, _):
        other = lax.rem(me + n, NB)
        pltpu.make_async_remote_copy(src_ref=dz.at[other], dst_ref=oq_ref.at[me], send_sem=x_send.at[0],
                                     recv_sem=x_recv.at[0], device_id={"outer": other // 16, "inner": lax.rem(other, 16)},
                                     device_id_type=MESH).start()
        return 0
    lax.fori_loop(1, NB, rows, 0)
    own_r = pltpu.make_async_copy(dz.at[me], oq_ref.at[me], own_sem.at[1])
    own_r.start()
    wait_bytes(from_a.at[0], a_recv.at[2])
    wait_bytes(from_a.at[1], a_recv.at[3])

    def strip(b):
        n = turn(be, b)
        return line[n] + from_a[0, n].astype(F32) + from_a[1, n].astype(F32)
    mid[0] = strip(2).astype(BF16)
    remote(mid.at[0, 0], opp_b.at[0], b_send.at[0], b_recv.at[0], to(0, 1))
    remote(mid.at[0, 1], opp_b.at[1], b_send.at[1], b_recv.at[1], to(0, -1))
    up, down, here = strip(1), strip(-1), strip(0)
    wait_bytes(opp_b.at[0], b_recv.at[0])
    mid[1, 0] = (up[0] + opp_b[0].astype(F32)).astype(BF16)
    mid[1, 1] = up[1].astype(BF16)
    remote(mid.at[1], from_b.at[0], b_send.at[2], b_recv.at[2], to(0, 1))
    wait_bytes(opp_b.at[1], b_recv.at[1])
    mid[2, 0] = down[0].astype(BF16)
    mid[2, 1] = (down[1] + opp_b[1].astype(F32)).astype(BF16)
    remote(mid.at[2], from_b.at[1], b_send.at[3], b_recv.at[3], to(0, -1))
    wait_bytes(from_b.at[0], b_recv.at[2])
    wait_bytes(from_b.at[1], b_recv.at[3])
    fin[...] = total(here, from_b[0], from_b[1]).astype(BF16)

    def strips(n, _):
        other = lax.rem(z + n, 8)
        pltpu.make_async_remote_copy(src_ref=fin.at[:, pl.ds(pl.multiple_of(other * 32, 32), 32)], dst_ref=okv_ref.at[z],
                                     send_sem=z_send.at[1], recv_sem=z_recv.at[1], device_id={"head": other},
                                     device_id_type=MESH).start()
        return 0
    lax.fori_loop(1, 8, strips, 0)
    own_k = pltpu.make_async_copy(fin.at[:, pl.ds(pl.multiple_of(z * 32, 32), 32)], okv_ref.at[z], own_sem.at[2])
    own_k.start()
    for c in started:
        c.wait_send()
    wait_bytes(dz.at[:, pl.ds(0, 7)], z_send.at[0])
    wait_bytes(oq_ref.at[pl.ds(0, NB - 1)], x_send.at[0])
    wait_bytes(oq_ref.at[pl.ds(0, NB - 1)], x_recv.at[0])
    wait_bytes(okv_ref.at[pl.ds(0, 7)], z_send.at[1])
    wait_bytes(okv_ref.at[pl.ds(0, 7)], z_recv.at[1])
    own_r.wait()
    own_k.wait()


def collect(dq, dkv):
    vm = pl.BlockSpec(memory_space=pltpu.VMEM)
    dma = pltpu.SemaphoreType.DMA
    block = (2, RB, HD)
    return pl.pallas_call(
        collect_kernel,
        out_shape=(jax.ShapeDtypeStruct((NB, 8, 8, HD), BF16), jax.ShapeDtypeStruct((8, 2, 32, HD), BF16)),
        in_specs=[vm] * 2, out_specs=(vm,) * 2,
        scratch_shapes=[
            pltpu.VMEM((4, 4) + block, BF16), pltpu.VMEM((3, 4) + block, BF16), pltpu.VMEM((2, 4) + block, BF16),
            pltpu.VMEM((2, 4, RB, HD), BF16), pltpu.VMEM((4,) + block, F32), pltpu.VMEM((2,) + block, BF16),
            pltpu.VMEM((2, RB, HD), BF16), pltpu.VMEM((3,) + block, BF16), pltpu.VMEM(block, BF16),
            pltpu.VMEM((NB, 8, 8, HD), BF16),
            dma((4,)), dma((4,)), dma((4,)), dma((4,)), dma((4,)), dma((4,)), dma((2,)), dma((2,)), dma((1,)), dma((1,)),
            dma((3,))],
        compiler_params=pltpu.CompilerParams(collective_id=1, has_side_effects=True, vmem_limit_bytes=48 << 20),
        name="collect",
    )(dq, dkv)


OI = ("outer", "inner")


def body(query, keys, values, forward_output, d_out, span_order):
    inv = jnp.zeros((NB,), jnp.int32).at[span_order[0]].set(jnp.arange(NB, dtype=jnp.int32))
    me = (lax.axis_index("outer") * 16 + lax.axis_index("inner")).astype(jnp.int32).reshape(1)
    delta = jnp.sum(d_out.astype(F32) * forward_output.astype(F32), axis=-1)
    delta = jnp.transpose(delta.reshape(8, NB, 8), (1, 0, 2)).reshape(NB, 1, PIECE)
    delta = jnp.pad(delta, ((0, 0), (0, 0), (0, 128 - PIECE)))
    kv, q, do, dl = spread(keys.reshape(RB, HD), values.reshape(RB, HD), query.reshape(8, NB, 8, HD),
                           d_out.reshape(8, NB, 8, HD), delta)
    dq, dkv = grads("T", inv, me, q, do, dl, kv)
    oq, okv = collect(dq.reshape(NB, 8, 8, HD), dkv)
    okv = jnp.transpose(okv, (1, 2, 0, 3))
    return oq.reshape(1, 32, 64, HD), okv[0][None], okv[1][None]


def solution(mesh):
    rows = P(OI, "head", None)
    out = P(OI, "head", None, None)
    return jax.shard_map(body, mesh=mesh, in_specs=(rows,) * 5 + (P(),), out_specs=(out,) * 3, check_vma=False)
```

profile of v0, /device:TPU:6, one launch (start us, length us, event | category | flops | bytes accessed | tf_op | source)
XLA Modules:
  0.0 197.5 jit_solution(13873547057648068929)
XLA Ops:
  0.6 0.7 fusion
  1.3 1.2 scatter_custom_fusion.inv
  2.5 1.5 multiply_reduce_fusion
  4.0 0.1 copy.16
  4.1 0.1 copy.17
  4.2 0.0 copy-start.2
  4.2 1.0 copy-done.2
  5.3 0.0 copy-start.6
  5.3 1.0 copy-done.6
  6.3 0.0 copy-start.7
  6.3 0.8 copy-done.7
  7.1 0.0 copy-start.8
  7.1 0.8 copy-done.8
  8.0 34.6 %spread.1 = (bf16[32,2,256,128]{3,2,1,0:T(8,128)(2,1)S(1)}, bf16[32,8,8,128]{3,2,1,0:T(8,128)(2,1)S(1)}, bf16[32,8,8,128]{3,2,1,0:T(8,128)(2,1)S(1)}, f32[32,1,128]{2,1,0:T(1,128)S(1)}) custom-call(bf16[256,128]{1,0:T(8,128)(2,1)S(1)} %bitcast.23, bf16[256,128]{1,0:T(8,128)(2,1)S(1)} %bitcast.24, bf16[8,32,8,128]{3,2,1,0:T(8,128)(2,1)S(1)} %bitcast.20, ...), custom_call_target="tpu_custom_call" | custom-call | tf_op jit(solution)/shard_map/spread/pallas_call | solution.py:295
  42.6 0.0 copy-start.1
  42.6 1.9 copy-done.1
  44.5 0.0 copy-start.4
  44.5 0.8 copy-done.4
  45.3 0.0 copy-start.5
  45.3 0.8 copy-done.5
  46.2 0.0 copy-start.9
  46.2 0.6 copy-done.9
  46.8 103.3 %grads_T.1 = (bf16[32,64,128]{2,1,0:T(8,128)(2,1)}, bf16[32,2,256,128]{3,2,1,0:T(8,128)(2,1)}) custom-call(s32[32]{0:T(128)} %scatter_custom_fusion.inv, s32[1]{0:T(128)} %bitcast.2.me_ref, bf16[32,8,8,128]{3,2,1,0:T(8,128)(2,1)} %copy-done.4, bf16[32,8,8,128]{3,2,1,0:T(8,128)(2,1)} %copy-done.5, f32[32,1,128]{2,1,0:T(1,128)} %copy-done.9, ...), custom_call_target="tpu_custom_call" | custom-call | tf_op jit(solution)/shard_map/grads_T/pallas_call | solution.py:128
  150.1 0.0 copy-start
  150.1 2.2 %copy-done = bf16[32,2,256,128]{3,2,1,0:T(8,128)(2,1)S(1)} copy-done((bf16[32,2,256,128]{3,2,1,0:T(8,128)(2,1)S(1)}, bf16[32,2,256,128]{3,2,1,0:T(8,128)(2,1)}, u32[]{:S(2)}) %copy-start) | copy-done | bytes 4194328
  152.2 0.0 copy-start.3
  152.2 1.0 copy-done.3
  153.3 42.1 %collect.1 = (bf16[32,8,8,128]{3,2,1,0:T(8,128)(2,1)S(1)}, bf16[8,2,32,128]{3,2,1,0:T(8,128)(2,1)S(1)}) custom-call(bf16[32,8,8,128]{3,2,1,0:T(8,128)(2,1)S(1)} %bitcast.19, bf16[32,2,256,128]{3,2,1,0:T(8,128)(2,1)S(1)} %copy-done), custom_call_target="tpu_custom_call" | custom-call | tf_op jit(solution)/shard_map/collect/pallas_call | solution.py:420
  195.4 0.7 copy.19
  196.0 0.7 copy.18
  196.7 0.8 copy.23
  (3 shorter events, 0.0 us)
Async XLA Ops:
  4.2 1.0 copy-start.2
  5.3 1.0 copy-start.6
  6.3 0.8 copy-start.7
  7.1 0.8 copy-start.8
  42.6 1.9 copy-start.1
  44.5 0.8 copy-start.4
  45.3 0.8 copy-start.5
  46.2 0.6 copy-start.9
  150.1 2.2 %copy-start = (bf16[32,2,256,128]{3,2,1,0:T(8,128)(2,1)S(1)}, bf16[32,2,256,128]{3,2,1,0:T(8,128)(2,1)}, u32[]{:S(2)}) copy-start(bf16[32,2,256,128]{3,2,1,0:T(8,128)(2,1)} %get-tuple-element.16.dkv_ref) | copy-start | bytes 12582916
  152.2 1.0 copy-start.3
where the time goes:
time: 198 us; the launch traced here: 197 us
  Pallas kernels  180 us (91%)
  local copies, waits for them, and re-layouts  14.6 us (7%)
  other arithmetic  2.21 us (1%)
    pallas_call x1, Pallas kernels, grads(): pl.pallas_call(functools.partial(grads_kernel, variant), out_shape=(jax.S...  103 us
    pallas_call x1, Pallas kernels, collect(): pl.pallas_call(collect_kernel, out_shape=(jax.ShapeDtypeStruct((NB, 8, 8,...  42.1 us
    pallas_call x1, Pallas kernels, spread(): pl.pallas_call(spread_kernel, out_shape=(jax.ShapeDtypeStruct((NB, 2, RB,...  34.6 us
    unnamed x23, local copies, waits for them, and re-layouts  13.3 us

commit v1 on v0

--- a/solution.py
+++ b/solution.py
@@ -1,5 +1,3 @@
-import functools
-
 import jax
 import jax.numpy as jnp
 from jax import lax
@@ -7,7 +5,7 @@
 from jax.experimental.pallas import tpu as pltpu
 from jax.sharding import PartitionSpec as P
 
-NB, RB, HD, PIECE, QC = 32, 256, 128, 64, 256
+NB, RB, HD, PIECE, QC, KEYS = 32, 256, 128, 64, 512, 4
 NG = NB * PIECE // QC
 PER = QC // PIECE
 NT = (((1,), (1,)), ((), ()))
@@ -41,103 +39,118 @@
     return u + shift <= row
 
 
-def grads_kernel(variant, inv, me_ref, q_ref, do_ref, dl_ref, kv_ref, dq_ref, dkv_ref,
-                 qpos, dopos, dlpos, lse, dqacc, dkacc, dvacc):
-    me = me_ref[0]
+def grads_kernel(order, q_ref, do_ref, dl_ref, kv_ref, dq_ref, dkv_ref,
+                 qpos, dopos, dlpos, lse, dqacc, kpos, vpos, dkacc, dvacc, inv):
+    me = lax.axis_index("outer") * 16 + lax.axis_index("inner")
+    for c in range(NB):
+        inv[order[c]] = c
     fill_positions(inv, q_ref, do_ref, dl_ref, qpos, dopos, dlpos)
+    for p in range(NB):
+        c = slot_of(inv[p])
+        kpos[p * RB:(p + 1) * RB, :] = kv_ref[c, 0]
+        vpos[p * RB:(p + 1) * RB, :] = kv_ref[c, 1]
+
+    def keys_at(ref, p, count):
+        return ref[pl.ds(pl.multiple_of(p * RB, RB), count * RB), :]
 
     def fold(state, s):
         m, l = state
-        s3 = s.reshape(s.shape[0] // 8, 8, QC)
+        s3 = s.reshape(s.shape[0] // 8, 8, s.shape[1])
         mn = jnp.maximum(m, jnp.max(s3, axis=0))
-        l = l * jnp.exp2(m - mn) + jnp.sum(jnp.exp2(s3 - mn[None]), axis=0)
+        low = mn * SCALE2
+        l = l * jnp.exp2(m * SCALE2 - low) + jnp.sum(jnp.exp2(s3 * SCALE2 - low[None]), axis=0)
         return mn, l
 
     def chunk_total(g, _):
         qg = qpos[pl.ds(pl.multiple_of(g * QC, QC), QC), :]
         state = (jnp.full((8, QC), NEG, F32), jnp.zeros((8, QC), F32))
 
-        def four(t, state):
-            for e in range(PER):
-                state = fold(state, dot(kv_ref[slot_of(inv[t * PER + e]), 0], qg, NT) * SCALE2)
-            return state
-        state = lax.fori_loop(0, g, four, state)
-        for e in range(PER):
-            s = dot(kv_ref[slot_of(inv[g * PER + e]), 0], qg, NT) * SCALE2
+        def some(t, state):
+            return fold(state, dot(keys_at(kpos, t * KEYS, KEYS), qg, NT))
+        state = lax.fori_loop(0, g * PER // KEYS, some, state)
+        half = PER // 2
+        for e in range(0, half, KEYS):
+            s = dot(keys_at(kpos, g * PER + e, KEYS), qg, NT)
             state = fold(state, jnp.where(make_visible(me, s.shape, e * RB), s, NEG))
+
+        def settle(m, l):
+            top = jnp.max(m, axis=0, keepdims=True)
+            return top * SCALE2 + jnp.log2(jnp.sum(l * jnp.exp2((m - top) * SCALE2), axis=0, keepdims=True))
         m, l = state
-        top = jnp.max(m, axis=0, keepdims=True)
-        lse[g] = top + jnp.log2(jnp.sum(l * jnp.exp2(m - top), axis=0, keepdims=True))
+        lse[g, :, :QC // 2] = settle(m[:, :QC // 2], l[:, :QC // 2])
+        state = (m[:, QC // 2:], l[:, QC // 2:])
+        for e in range(0, half, KEYS):
+            s = dot(keys_at(kpos, g * PER + half + e, KEYS), qg[QC // 2:], NT)
+            state = fold(state, jnp.where(make_visible(me, s.shape, e * RB), s, NEG))
+        lse[g, :, QC // 2:] = settle(*state)
         return 0
     lax.fori_loop(0, NG, chunk_total, 0)
 
     dqacc[...] = jnp.zeros_like(dqacc)
 
-    def key_block(p, _):
-        c = slot_of(inv[p])
-        kb, vb = kv_ref[c, 0], kv_ref[c, 1]
+    def key_block(t, _):
+        p = t * KEYS
+        kb, vb = keys_at(kpos, p, KEYS), keys_at(vpos, p, KEYS)
         first = p // PER
-        if variant == "T":
-            kt = kb.T
-
-        def visit(g, masked):
-            rows = pl.ds(pl.multiple_of(g * QC, QC), QC)
+        kt = kb.T
+
+        def visit(g, lo, masked):
+            rows = pl.ds(pl.multiple_of(g * QC + lo, QC // 2), QC - lo)
             qg, dog = qpos[rows, :], dopos[rows, :]
-            s = dot(kb, qg, NT) * SCALE2 - lse[g]
+            s = dot(kb, qg, NT) * SCALE2 - lse[g, :, lo:]
             w = jnp.exp2(s)
             if masked:
-                w = jnp.where(make_visible(me, s.shape, (p - g * PER) * RB), w, 0.0)
+                w = jnp.where(make_visible(me, s.shape, 0), w, 0.0)
             dv = dot(w.astype(BF16), dog, NN)
-            ds = (w * (dot(vb, dog, NT) - dlpos[g])).astype(BF16)
+            ds = (w * (dot(vb, dog, NT) - dlpos[g, :, lo:])).astype(BF16)
             dk = dot(ds, qg, NN)
-            if variant == "T":
-                dqacc[g] += dot(kt, ds, NN)
-            else:
-                dqacc[g] += dot(ds, kb, TN)
+            dqacc[g, :, lo:] += dot(kt, ds, NN)
             return dk, dv
-        dk, dv = visit(first, True)
-        dkacc[...] = dk
-        dvacc[...] = dv
+
+        @pl.when(t % 2 == 0)
+        def _():
+            dkacc[...], dvacc[...] = visit(first, 0, True)
+
+        @pl.when(t % 2 == 1)
+        def _():
+            dkacc[...], dvacc[...] = visit(first, QC // 2, True)
 
         def rest(g, _):
-            dk, dv = visit(g, False)
+            dk, dv = visit(g, 0, False)
             dkacc[...] += dk
             dvacc[...] += dv
             return 0
         lax.fori_loop(first + 1, NG, rest, 0)
-        dkv_ref[c, 0] = (dkacc[...] * SCALE).astype(BF16)
-        dkv_ref[c, 1] = dvacc[...].astype(BF16)
-        return 0
-    lax.fori_loop(0, NB, key_block, 0)
+        for e in range(KEYS):
+            c = slot_of(inv[p + e])
+            dkv_ref[c, 0] = (dkacc[e * RB:(e + 1) * RB, :] * SCALE).astype(BF16)
+            dkv_ref[c, 1] = dvacc[e * RB:(e + 1) * RB, :].astype(BF16)
+        return 0
+    lax.fori_loop(0, NB // KEYS, key_block, 0)
 
     for p in range(NB):
         g, e = divmod(p, PER)
-        if variant == "T":
-            if e == 0:
-                whole = dqacc[g].T
-            part = whole[e * PIECE:(e + 1) * PIECE, :]
-        else:
-            part = dqacc[g, e * PIECE:(e + 1) * PIECE, :]
-        dq_ref[inv[p]] = (part * SCALE).astype(BF16)
-
-
-def grads(variant, inv, me, q, do, dl, kv):
-    acc = (NG, HD, QC) if variant == "T" else (NG, QC, HD)
+        if e == 0:
+            whole = dqacc[g].T
+        dq_ref[inv[p]] = (whole[e * PIECE:(e + 1) * PIECE, :] * SCALE).astype(BF16)
+
+
+def grads(order, q, do, dl, kv):
     vm = pl.BlockSpec(memory_space=pltpu.VMEM)
     sm = pl.BlockSpec(memory_space=pltpu.SMEM)
     return pl.pallas_call(
-        functools.partial(grads_kernel, variant),
-        out_shape=(jax.ShapeDtypeStruct((NB, PIECE, HD), BF16),
-                   jax.ShapeDtypeStruct((NB, 2, RB, HD), BF16)),
-        in_specs=[sm, sm, vm, vm, vm, vm],
+        grads_kernel,
+        out_shape=(jax.ShapeDtypeStruct((NB, PIECE, HD), BF16), jax.ShapeDtypeStruct((NB, 2, RB, HD), BF16)),
+        in_specs=[sm, vm, vm, vm, vm],
         out_specs=(vm, vm),
         scratch_shapes=[
             pltpu.VMEM((NB * PIECE, HD), BF16), pltpu.VMEM((NB * PIECE, HD), BF16), pltpu.VMEM((NG, 1, QC), F32),
-            pltpu.VMEM((NG, 1, QC), F32), pltpu.VMEM(acc, F32),
-            pltpu.VMEM((RB, HD), F32), pltpu.VMEM((RB, HD), F32)],
-        compiler_params=pltpu.CompilerParams(vmem_limit_bytes=60 << 20),
-        name="grads_" + variant,
-    )(inv, me, q, do, dl, kv)
+            pltpu.VMEM((NG, 1, QC), F32), pltpu.VMEM((NG, HD, QC), F32),
+            pltpu.VMEM((NB * RB, HD), BF16), pltpu.VMEM((NB * RB, HD), BF16),
+            pltpu.VMEM((KEYS * RB, HD), F32), pltpu.VMEM((KEYS * RB, HD), F32), pltpu.SMEM((NB,), jnp.int32)],
+        compiler_params=pltpu.CompilerParams(vmem_limit_bytes=40 << 20),
+        name="grads",
+    )(order, q, do, dl, kv)
 
 
 MESH = pl.DeviceIdType.MESH
@@ -296,9 +309,9 @@
         spread_kernel,
         out_shape=(jax.ShapeDtypeStruct((NB, 2, RB, HD), BF16), jax.ShapeDtypeStruct((NB, 8, 8, HD), BF16),
                    jax.ShapeDtypeStruct((NB, 8, 8, HD), BF16), jax.ShapeDtypeStruct((NB, 1, HD), F32)),
-        in_specs=[vm] * 5, out_specs=(vm,) * 4,
+        in_specs=[pl.BlockSpec(memory_space=pltpu.HBM)] * 4 + [vm], out_specs=(vm,) * 4,
         scratch_shapes=[dma((20,)), dma((20,)), dma((16,)), dma((16,)), dma((3,)), dma((3,)), dma((5,))],
-        compiler_params=pltpu.CompilerParams(collective_id=0, has_side_effects=True, vmem_limit_bytes=40 << 20),
+        compiler_params=pltpu.CompilerParams(collective_id=0, has_side_effects=True, vmem_limit_bytes=16 << 20),
         name="spread",
     )(k, v, q, do, dl)
 
@@ -428,7 +441,7 @@
             pltpu.VMEM((NB, 8, 8, HD), BF16),
             dma((4,)), dma((4,)), dma((4,)), dma((4,)), dma((4,)), dma((4,)), dma((2,)), dma((2,)), dma((1,)), dma((1,)),
             dma((3,))],
-        compiler_params=pltpu.CompilerParams(collective_id=1, has_side_effects=True, vmem_limit_bytes=48 << 20),
+        compiler_params=pltpu.CompilerParams(collective_id=1, has_side_effects=True, vmem_limit_bytes=40 << 20),
         name="collect",
     )(dq, dkv)
 
@@ -437,14 +450,12 @@
 
 
 def body(query, keys, values, forward_output, d_out, span_order):
-    inv = jnp.zeros((NB,), jnp.int32).at[span_order[0]].set(jnp.arange(NB, dtype=jnp.int32))
-    me = (lax.axis_index("outer") * 16 + lax.axis_index("inner")).astype(jnp.int32).reshape(1)
     delta = jnp.sum(d_out.astype(F32) * forward_output.astype(F32), axis=-1)
     delta = jnp.transpose(delta.reshape(8, NB, 8), (1, 0, 2)).reshape(NB, 1, PIECE)
     delta = jnp.pad(delta, ((0, 0), (0, 0), (0, 128 - PIECE)))
     kv, q, do, dl = spread(keys.reshape(RB, HD), values.reshape(RB, HD), query.reshape(8, NB, 8, HD),
                            d_out.reshape(8, NB, 8, HD), delta)
-    dq, dkv = grads("T", inv, me, q, do, dl, kv)
+    dq, dkv = grads(span_order[0], q, do, dl, kv)
     oq, okv = collect(dq.reshape(NB, 8, 8, HD), dkv)
     okv = jnp.transpose(okv, (1, 2, 0, 3))
     return oq.reshape(1, 32, 64, HD), okv[0][None], okv[1][None]

time: 198 us -> 132 us (0.67)
  Pallas kernels: 180 us -> 123 us
  local copies, waits for them, and re-layouts: 14.6 us -> 6.71 us
    pallas_call x1, Pallas kernels: 103 us -> 45.8 us  [grads(): pl.pallas_call(grads_kernel, out_shape=(jax.ShapeDtypeStruct((NB, PIECE,...]
    unnamed x23 -> x13, local copies, waits for them, and re-layouts: 13.3 us -> 6.51 us
where the time goes in v1:
time: 132 us
  Pallas kernels  123 us (93%)
  local copies, waits for them, and re-layouts  6.71 us (5%)
  other arithmetic  1.55 us (1%)
    pallas_call x1, Pallas kernels, grads(): pl.pallas_call(grads_kernel, out_shape=(jax.ShapeDtypeStruct((NB, PIECE,...  45.8 us
    pallas_call x1, Pallas kernels, collect(): pl.pallas_call(collect_kernel, out_shape=(jax.ShapeDtypeStruct((NB, 8, 8,...  42.4 us
    pallas_call x1, Pallas kernels, spread(): pl.pallas_call(spread_kernel, out_shape=(jax.ShapeDtypeStruct((NB, 2, RB,...  34.6 us
    unnamed x13, local copies, waits for them, and re-layouts  6.51 us

profile of v1, /device:TPU:6, one launch (start us, length us, event | category | flops | bytes accessed | tf_op | source)
XLA Modules:
  0.0 131.8 jit_solution(7855035890339674206)
XLA Ops:
  0.6 1.5 %multiply_reduce_fusion = f32[256,8]{1,0:T(8,128)S(1)} fusion(bf16[256,8,128]{2,1,0:T(8,128)(2,1)} %param.9, bf16[256,8,128]{2,1,0:T(8,128)(2,1)} %param.10), kind=kLoop, calls=%fused_computation | loop fusion | flops 1046528 | bytes 1056768 | tf_op jit(solution)/shard_map/reduce_sum | solution.py:453
  2.2 0.1 copy.16
  2.3 0.1 copy.17
  2.4 0.0 copy-start
  2.4 1.0 copy-done
  3.4 0.0 copy-start.1
  3.4 1.0 copy-done.1
  4.5 0.0 copy-start.2
  4.5 0.8 copy-done.2
  5.3 0.0 copy-start.3
  5.3 0.8 copy-done.3
  6.1 34.6 %spread.1 = (bf16[32,2,256,128]{3,2,1,0:T(8,128)(2,1)S(1)}, bf16[32,8,8,128]{3,2,1,0:T(8,128)(2,1)S(1)}, bf16[32,8,8,128]{3,2,1,0:T(8,128)(2,1)S(1)}, f32[32,1,128]{2,1,0:T(1,128)S(1)}) custom-call(bf16[256,128]{1,0:T(8,128)(2,1)S(1)} %bitcast.18, bf16[256,128]{1,0:T(8,128)(2,1)S(1)} %bitcast.19, bf16[8,32,8,128]{3,2,1,0:T(8,128)(2,1)S(1)} %bitcast.15, ...), custom_call_target="tpu_custom_call" | custom-call | tf_op jit(solution)/shard_map/spread/pallas_call | solution.py:308
  40.7 0.0 copy-start.4
  40.8 0.6 copy-done.4
  41.4 45.8 %grads.1 = (bf16[32,64,128]{2,1,0:T(8,128)(2,1)S(1)}, bf16[32,2,256,128]{3,2,1,0:T(8,128)(2,1)S(1)}) custom-call(s32[32]{0:T(128)S(1)} %bitcast.20, bf16[32,8,8,128]{3,2,1,0:T(8,128)(2,1)S(1)} %get-tuple-element.11.q_ref, bf16[32,8,8,128]{3,2,1,0:T(8,128)(2,1)S(1)} %get-tuple-element.12.do_ref, f32[32,1,128]{2,1,0:T(1,128)S(1)} %get-tuple-element.13.dl_ref, ...), custom_call_target="tpu_custom_call" | custom-call | tf_op jit(solution)/shard_map/grads/pallas_call | solution.py:141
  87.2 42.4 %collect.1 = (bf16[32,8,8,128]{3,2,1,0:T(8,128)(2,1)S(1)}, bf16[8,2,32,128]{3,2,1,0:T(8,128)(2,1)S(1)}) custom-call(bf16[32,8,8,128]{3,2,1,0:T(8,128)(2,1)S(1)} %bitcast.14, bf16[32,2,256,128]{3,2,1,0:T(8,128)(2,1)S(1)} %get-tuple-element.16.dkv_ref), custom_call_target="tpu_custom_call" | custom-call | tf_op jit(solution)/shard_map/collect/pallas_call | solution.py:433
  129.7 0.7 copy.19
  130.4 0.7 copy.18
  131.0 0.8 copy.23
  (2 shorter events, 0.0 us)
Async XLA Ops:
  2.4 1.0 copy-start
  3.4 1.0 copy-start.1
  4.5 0.8 copy-start.2
  5.3 0.8 copy-start.3
  40.7 0.7 copy-start.4
